TPU v7x, 128 devices: a whole 4x4x4 slice. The times are simulated.
128 devices in a mesh: layer: 2 (over core), latent: 64 (over y, x, z).
Axes of the slice: x: 4, y: 4, z: 4, core: 2. Of those that a mesh axis runs over, the one named last changes fastest.
Arguments:
- activations: bfloat16 [2, 512, 2048], P('layer', 'latent'), may hold values from -15 to 15
- enc_weight: bfloat16 [2, 2048, 65536], P('layer', None, 'latent'), may hold values from -0.09375 to 0.09375
- enc_bias: float32 [65536], P('latent'), may hold values from -3 to 3
- dec_weight: bfloat16 [2, 65536, 2048], P('layer', 'latent'), may hold values from -0.08984375 to 0.08984375
- dec_bias: float32 [2, 2048], P('layer'), may hold values from -3 to 3
- active_mask: int32 [512, 65536], P(None, 'latent'), may hold values 0 or 1
Outputs:
- grad_enc: bfloat16 [2, 2048, 65536], P('layer', None, 'latent')
- grad_dec: bfloat16 [2, 65536, 2048], P('layer', 'latent')
- loss_value: float32 [], replicated
All inputs are finite; a program needn't handle non-finite values. No bound on the sum of `active_mask` on one device may be relied on, other than what follows from the above.
Results may differ from a plain program's by a relative error of at most 0.0065.
Values may be sent and summed in bfloat16 or wider, within the bound.
No kernel may reach another device: no remote copies, remote signals or barrier semaphores. Data moves between devices by JAX's collectives and lax.ppermute only.
A program may use at most 128 MiB of HBM per device.

v0:
```python
import jax
import jax.numpy as jnp
from jax import lax
from jax.sharding import Mesh
from jax.sharding import PartitionSpec as P

LATENT = ("latent_0", "latent_1", "latent_2")
LAYER_LATENT = ("layer", "latent_0", "latent_1", "latent_2")
sparsity_weight = 0.4


def sent_to_all(x, axis):
    count = lax.axis_size(axis)
    return lax.all_to_all(jnp.broadcast_to(x[None], (count, *x.shape)), axis, 0, 0, tiled=True)


def joined_along(blocks, dim):
    blocks = jnp.moveaxis(blocks, 0, dim)
    shape = blocks.shape
    return blocks.reshape(*shape[:dim], shape[dim] * shape[dim + 1], *shape[dim + 2 :])


def collect(x, axis, dim):
    blocks = sent_to_all(x, axis)
    return joined_along(blocks, dim)


def over_axes(x, axes):
    for axis in axes:
        x = lax.psum(x, axis)
    return x


def per_device(activations, enc_weight, enc_bias, dec_weight, dec_bias, active_mask):
    local_rows = activations[0]
    encoder = enc_weight[0]
    decoder = dec_weight[0]
    token_all = collect(local_rows, LATENT, 0)
    layer_pre = jnp.dot(token_all, encoder, preferred_element_type=jnp.float32)
    dec_float = decoder.astype(jnp.float32)
    row_norm = jnp.sqrt(jnp.sum(dec_float * dec_float, axis=1) + 1e-06)
    preact, norm_sum = lax.psum((layer_pre, row_norm), "layer")
    preact = preact + enc_bias
    gating = active_mask.astype(jnp.float32)
    latent_code = preact * gating
    code_b = latent_code.astype(jnp.bfloat16)
    layer_index = lax.axis_index("layer")
    latent_index = lax.axis_index(LATENT)
    partial_value = jnp.dot(code_b, decoder, preferred_element_type=jnp.float32)
    recon = lax.psum(partial_value, LATENT) + dec_bias[0]
    error_full = recon - token_all.astype(jnp.float32)
    error_b = error_full.astype(jnp.bfloat16)
    square_part = jnp.where(latent_index == 0, 0.5 * jnp.sum(error_full * error_full), 0.0)
    layer_grad = jnp.einsum("td,fd->tf", error_b, decoder, preferred_element_type=jnp.float32)
    code_grad = lax.psum(layer_grad, "layer") + sparsity_weight * norm_sum
    preact_grad = (code_grad * gating).astype(jnp.bfloat16)
    grad_enc = jnp.einsum(
        "td,tf->df", token_all, preact_grad, preferred_element_type=jnp.float32
    ).astype(jnp.bfloat16)
    code_total = jnp.sum(latent_code, axis=0)
    shrink = sparsity_weight * code_total[:, None] * dec_float / row_norm[:, None]
    grad_dec = (
        jnp.einsum("tf,td->fd", code_b, error_b, preferred_element_type=jnp.float32) + shrink
    ).astype(jnp.bfloat16)
    sparse_part = jnp.where(
        layer_index == 0, sparsity_weight * jnp.sum(latent_code * norm_sum), 0.0
    )
    loss_total = over_axes(square_part + sparse_part, LAYER_LATENT)
    loss_value = loss_total / (active_mask.shape[0] * token_all.shape[1])
    return (grad_enc[None], grad_dec[None], loss_value)


def solution(mesh):
    torus = Mesh(
        mesh.devices.reshape(mesh.shape["layer"], 4, 4, 4),
        ("layer", "latent_0", "latent_1", "latent_2"),
    )
    placed = (
        P("layer", LATENT, None),
        P("layer", None, LATENT),
        P(LATENT),
        P("layer", LATENT, None),
        P("layer", None),
        P(None, LATENT),
    )
    return jax.shard_map(
        per_device,
        mesh=torus,
        in_specs=placed,
        out_specs=(P("layer", None, LATENT), P("layer", LATENT, None), P()),
        check_vma=False,
    )
```

profile of v0, /device:TPU:0, one launch (start us, length us, event | category | flops | bytes accessed | tf_op | source)
XLA Modules:
  0.0 295.7 jit_solution(14618392666978174406)
XLA Ops:
  7.2 0.0 all-reduce.4.cloned.1.call-start
  7.2 1.0 broadcast_in_dim.9
  8.2 0.0 copy-start.5
  8.2 41.2 %all_to_all.5 = bf16[64,8,2048]{2,1,0:T(8,128)(2,1)S(1)} all-to-all(bf16[64,8,2048]{2,1,0:T(8,128)(2,1)S(1)} %broadcast_in_dim.9), channel_id=1, replica_groups=mesh['layer'=2,'latent_0'=4,'latent_1'=4,'latent_2'=4] {'latent_0','late..., dimensions={0} | all-to-all | bytes 4194304 | tf_op jit(solution)/shard_map/all_to_all | solution.py:14
  49.4 0.0 copy-done.5
  49.4 3.7 %fusion.8 = f32[512,1024]{1,0:T(8,128)} fusion(bf16[1,2048,1024]{2,1,0:T(8,128)(2,1)S(1)} %copy-done.5, bf16[64,8,2048]{2,1,0:T(8,128)(2,1)S(1)} %all_to_all.5), kind=kOutput, calls=%fused_computation.10 | convolution fusion | flops 2147483648 | bytes 8388608 | tf_op jit(solution)/shard_map/dot_general | solution.py:39
  53.1 0.0 all-reduce.4.cloned.1.call-update
  53.1 0.0 copy-start.4
  53.1 0.0 all-reduce.6.cloned.1.call-start
  53.2 3.1 %fusion = f32[1024]{0:T(1024)S(1)} fusion(bf16[1,1024,2048]{2,1,0:T(8,128)(2,1)} %param.9), kind=kLoop, calls=%fused_computation.2 | loop fusion | flops 6290432 | bytes 4198400 | tf_op jit(solution)/shard_map/reduce_sum | solution.py:41
  56.3 2.5 psum.59
  58.8 17.8 %all-reduce.4.cloned.1.call-done = f32[512,1024]{1,0:T(8,128)} async-done(((f32[512,1024]{1,0:T(8,128)}), f32[512,1024]{1,0:T(8,128)}) %all-reduce.4.cloned.1.call-update) | async-done | bytes 2097168 | tf_op jit(solution)/shard_map/psum | solution.py:42
  76.5 0.0 copy-done.4
  76.5 3.6 %multiply_reduce_fusion.1 = (f32[]{:T(128)}, f32[1024]{0:T(1024)S(1)}, bf16[512,1024]{1,0:T(8,128)(2,1)S(1)}) fusion(f32[1024]{0:T(1024)S(1)} %psum.59, s32[512,1024]{1,0:T(8,128)} %param.11, f32[512,1024]{1,0:T(8,128)} %all-reduce.4.cloned.1.call-done, f32[1024]{0:T(1024)S(1)} %copy-done.4), kind=kLoop, calls=%fused_computation.19 | loop fusion | flops 3668991 | bytes 5255172 | tf_op jit(solution)/shard_map/reduce_sum | solution.py:66
  80.1 0.0 copy-done
  80.1 4.4 %fusion.6 = f32[512,2048]{1,0:T(8,128)} fusion(bf16[1,1024,2048]{2,1,0:T(8,128)(2,1)S(1)} %copy-done, bf16[512,1024]{1,0:T(8,128)(2,1)S(1)} %get-tuple-element.8), kind=kOutput, calls=%fused_computation.8 | convolution fusion | flops 2147483648 | bytes 9437184 | tf_op jit(solution)/shard_map/dot_general | solution.py:49
  84.5 0.0 all-reduce.6.cloned.1.call-update
  84.5 0.0 all-reduce.8.cloned.1.call-start
  84.6 140.1 %all-reduce.6.cloned.1.call-done = f32[512,2048]{1,0:T(8,128)} async-done(((f32[512,2048]{1,0:T(8,128)}), f32[512,2048]{1,0:T(8,128)}) %all-reduce.6.cloned.1.call-update) | async-done | bytes 4194320 | tf_op jit(solution)/shard_map/psum | solution.py:50
  224.7 0.0 copy-done.3
  224.7 4.0 %multiply_reduce_fusion = (f32[]{:T(128)}, bf16[512,2048]{1,0:T(8,128)(2,1)S(1)}) fusion(f32[512,2048]{1,0:T(8,128)} %all-reduce.6.cloned.1.call-done, bf16[64,8,2048]{2,1,0:T(8,128)(2,1)S(1)} %all_to_all.5, f32[2048]{0:T(1024)S(1)} %bitcast.32), kind=kLoop, calls=%fused_computation.12 | loop fusion | flops 6291455 | bytes 8396804 | tf_op jit(solution)/shard_map/reduce_sum | solution.py:53
  228.8 1.3 copy-done.2
  230.1 0.0 copy-done.1
  230.1 3.7 %fusion.4 = f32[512,1024]{1,0:T(8,128)} fusion(bf16[512,2048]{1,0:T(8,128)(2,1)S(1)} %get-tuple-element.10, bf16[1,1024,2048]{2,1,0:T(8,128)(2,1)S(1)} %copy-done.1), kind=kOutput, calls=%fused_computation.6 | convolution fusion | flops 2147483648 | bytes 8388608 | tf_op jit(solution)/shard_map/td,fd->tf/dot_general | solution.py:54
  233.8 0.0 all-reduce.8.cloned.1.call-update
  235.1 3.0 %psum.60 = f32[]{:T(128)} all-reduce(f32[]{:T(128)S(6)} %add.76), channel_id=1, replica_groups=mesh['layer'=2,'latent_0'=4,'latent_1'=4,'latent_2'=4] {'layer'}, use_global_device_ids=true, to_apply=%region_8.9 | all-reduce | flops 1 | bytes 8 | tf_op jit(solution)/shard_map/psum | solution.py:30
  238.1 9.3 %psum.61 = f32[]{:T(128)} all-reduce(f32[]{:T(128)} %psum.60), channel_id=1, replica_groups=mesh['layer'=2,'latent_0'=4,'latent_1'=4,'latent_2'=4] {'latent_0'}, use_global_device_ids=true, to_apply=%region_9.10 | all-reduce | flops 1 | bytes 8 | tf_op jit(solution)/shard_map/psum | solution.py:30
  247.4 10.7 %psum.62 = f32[]{:T(128)} all-reduce(f32[]{:T(128)} %psum.61), channel_id=1, replica_groups=mesh['layer'=2,'latent_0'=4,'latent_1'=4,'latent_2'=4] {'latent_1'}, use_global_device_ids=true, to_apply=%region_10.11 | all-reduce | flops 1 | bytes 8 | tf_op jit(solution)/shard_map/psum | solution.py:30
  258.1 9.6 %psum.63 = f32[]{:T(128)} all-reduce(f32[]{:T(128)} %psum.62), channel_id=1, replica_groups=mesh['layer'=2,'latent_0'=4,'latent_1'=4,'latent_2'=4] {'latent_2'}, use_global_device_ids=true, to_apply=%region_11.12 | all-reduce | flops 1 | bytes 8 | tf_op jit(solution)/shard_map/psum | solution.py:30
  268.3 6.7 %fusion.10 = bf16[1,1024,2048]{2,1,0:T(8,128)(2,1)} fusion(f32[1024]{0:T(1024)S(1)} %add_sqrt_fusion, bf16[1,1024,2048]{2,1,0:T(8,128)(2,1)} %param.9, f32[1024]{0:T(1024)S(1)} %broadcast_multiply_fusion, bf16[512,2048]{1,0:T(8,128)(2,1)} %copy-done.2, bf16[512,1024]{1,0:T(8,128)(2,1)S(1)} %get-tuple-element.8), kind=kOutput, calls=%fused_computation.15 | convolution fusion | flops 2157969408 | bytes 11542528 | tf_op jit(solution)/shard_map/tf,td->fd/dot_general | solution.py:63
  275.0 6.7 %convert_bitcast_fusion = bf16[1,2048,1024]{1,2,0:T(8,128)(2,1)} fusion(bf16[64,8,2048]{2,1,0:T(8,128)(2,1)S(1)} %all_to_all.5, f32[512,1024]{1,0:T(8,128)} %all-reduce.8.cloned.1.call-done, s32[512,1024]{1,0:T(8,128)} %param.11, f32[1024]{0:T(1024)S(1)} %broadcast_multiply_fusion.1), kind=kOutput, calls=%fused_computation.13 | convolution fusion | flops 2151677952 | bytes 10489856 | tf_op jit(solution)/shard_map/td,tf->df/dot_general | solution.py:57
  281.7 6.4 %copy.9 = bf16[1,2048,1024]{2,1,0:T(8,128)(2,1)} copy(bf16[1,2048,1024]{1,2,0:T(8,128)(2,1)} %convert_bitcast_fusion) | data formatting | bytes 8388608
  (8 shorter events, 0.0 us)
Async XLA Ops:
  7.2 69.4 %all-reduce.4.cloned.1.call-start = ((), (), s32[]{:S(2)}) async-start(), calls=%async_computation.1 | async-start | bytes 4194304 | tf_op jit(solution)/shard_map/psum | solution.py:42
  8.2 41.2 %copy-start.5 = (bf16[1,2048,1024]{2,1,0:T(8,128)(2,1)S(1)}, bf16[1,2048,1024]{2,1,0:T(8,128)(2,1)}, u32[]{:S(2)}) copy-start(bf16[1,2048,1024]{2,1,0:T(8,128)(2,1)} %param.7) | copy-start | bytes 12582916
  53.1 23.4 %copy-start.4 = (f32[1024]{0:T(1024)S(1)}, f32[1024]{0:T(1024)}, u32[]{:S(2)}) copy-start(f32[1024]{0:T(1024)} %param.8) | copy-start | bytes 12292
  53.1 171.6 %all-reduce.6.cloned.1.call-start = ((), (), s32[]{:S(2)}) async-start(), calls=%async_computation.2 | async-start | bytes 8388608 | tf_op jit(solution)/shard_map/psum | solution.py:50
  76.5 3.6 %copy-start = (bf16[1,1024,2048]{2,1,0:T(8,128)(2,1)S(1)}, bf16[1,1024,2048]{2,1,0:T(8,128)(2,1)}, u32[]{:S(2)}) copy-start(bf16[1,1024,2048]{2,1,0:T(8,128)(2,1)} %param.9) | copy-start | bytes 12582916
  84.5 140.2 %copy-start.3 = (f32[1,2048]{1,0:T(1,128)S(1)}, f32[1,2048]{1,0:T(1,128)}, u32[]{:S(2)}) copy-start(f32[1,2048]{1,0:T(1,128)} %param.10) | copy-start | bytes 24580
  84.5 190.4 %all-reduce.8.cloned.1.call-start = ((), (), s32[]{:S(2)}) async-start(), calls=%async_computation.3 | async-start | bytes 4194304 | tf_op jit(solution)/shard_map/psum | solution.py:55
  224.7 5.4 %copy-start.1 = (bf16[1,1024,2048]{2,1,0:T(8,128)(2,1)S(1)}, bf16[1,1024,2048]{2,1,0:T(8,128)(2,1)}, u32[]{:S(2)}) copy-start(bf16[1,1024,2048]{2,1,0:T(8,128)(2,1)} %param.9) | copy-start | bytes 12582916
  228.8 1.4 copy-start.2
Sparse Core Ops, SparseCore 0:
  53.3 23.2 all-reduce.3
  84.7 140.0 all-reduce.5
  234.0 24.1 all-reduce.7
where the time goes:
time: 296 us
  waiting for transfers between devices  158 us (53%)
  blocking collectives  76.2 us (26%)
  matrix products  25.1 us (8%)
  between operations  16.9 us (6%)
  other arithmetic  10.7 us (4%)
  local copies, waits for them, and re-layouts  8.76 us (3%)
    psum x1, waiting for transfers between devices, per_device(): recon = lax.psum(partial_value, LATENT) + dec_bias[0]  140 us
    all_to_all x1, blocking collectives, sent_to_all(): lax.all_to_all(jnp.broadcast_to(x[None], (count, *x.shape)), axis, 0, 0,...  41.2 us
    psum x4, blocking collectives, over_axes(): x = lax.psum(x, axis)  32.5 us
    psum x1, waiting for transfers between devices, per_device(): preact, norm_sum = lax.psum((layer_pre, row_norm), 'layer')  17.8 us
    unnamed x13, local copies, waits for them, and re-layouts  7.77 us
    dot_general x1, matrix products, per_device(): jnp.einsum('td,tf->df', token_all, preact_grad, preferred_element_type=jn...  6.68 us
    dot_general x1, matrix products, per_device(): jnp.einsum('tf,td->fd', code_b, error_b, preferred_element_type=jnp.float32)  6.65 us
  transfers between devices with their start and end apart: 3, of which 2 were waited for; matrix products, arithmetic and copies ran while one was open for 3% of the time, Pallas kernels for 0%

commit v1 on v0

--- a/solution.py
+++ b/solution.py
@@ -47,7 +47,7 @@
     layer_index = lax.axis_index("layer")
     latent_index = lax.axis_index(LATENT)
     partial_value = jnp.dot(code_b, decoder, preferred_element_type=jnp.float32)
-    recon = lax.psum(partial_value, LATENT) + dec_bias[0]
+    recon = lax.psum(lax.psum(partial_value, ("latent_1", "latent_2")), "latent_0") + dec_bias[0]
     error_full = recon - token_all.astype(jnp.float32)
     error_b = error_full.astype(jnp.bfloat16)
     square_part = jnp.where(latent_index == 0, 0.5 * jnp.sum(error_full * error_full), 0.0)

time: 296 us -> 358 us (1.21)
  waiting for transfers between devices: 158 us -> 218 us
    psum x1 -> x2, waiting for transfers between devices: 140 us -> 200 us  [the longest x1 105 us: per_device(): lax.psum(partial_value, ('latent_1', 'latent_2'))]
  transfers between devices with their start and end apart: 3 -> 4, of which waited for: 2 -> 3; matrix products, arithmetic and copies ran while one was open for 3% -> 3% of each run, Pallas kernels for 0% -> 0%
where the time goes in v1:
time: 358 us
  waiting for transfers between devices  218 us (61%)
  blocking collectives  78.3 us (22%)
  matrix products  25.1 us (7%)
  between operations  16.9 us (5%)
  other arithmetic  10.7 us (3%)
  local copies, waits for them, and re-layouts  8.76 us (2%)
    psum x1, waiting for transfers between devices, per_device(): lax.psum(partial_value, ('latent_1', 'latent_2'))  105 us
    psum x1, waiting for transfers between devices, per_device(): lax.psum(lax.psum(partial_value, ('latent_1', 'latent_2')), 'latent_0')  94.9 us
    all_to_all x1, blocking collectives, sent_to_all(): lax.all_to_all(jnp.broadcast_to(x[None], (count, *x.shape)), axis, 0, 0,...  41.2 us
    psum x4, blocking collectives, over_axes(): x = lax.psum(x, axis)  34.6 us
    psum x1, waiting for transfers between devices, per_device(): preact, norm_sum = lax.psum((layer_pre, row_norm), 'layer')  17.8 us
    unnamed x13, local copies, waits for them, and re-layouts  7.77 us
  transfers between devices with their start and end apart: 4, of which 3 were waited for; matrix products, arithmetic and copies ran while one was open for 3% of the time, Pallas kernels for 0%

profile of v1, /device:TPU:0, one launch (start us, length us, event | category | flops | bytes accessed | tf_op | source)
XLA Modules:
  0.0 357.7 jit_solution(16903480778219382350)
XLA Ops:
  7.2 0.0 all-reduce.5.cloned.1.call-start
  7.2 1.0 broadcast_in_dim.9
  8.2 0.0 copy-start.5
  8.2 41.2 %all_to_all.5 = bf16[64,8,2048]{2,1,0:T(8,128)(2,1)S(1)} all-to-all(bf16[64,8,2048]{2,1,0:T(8,128)(2,1)S(1)} %broadcast_in_dim.9), channel_id=1, replica_groups=mesh['layer'=2,'latent_0'=4,'latent_1'=4,'latent_2'=4] {'latent_0','late..., dimensions={0} | all-to-all | bytes 4194304 | tf_op jit(solution)/shard_map/all_to_all | solution.py:14
  49.4 0.0 copy-done.5
  49.4 3.7 %fusion.8 = f32[512,1024]{1,0:T(8,128)} fusion(bf16[1,2048,1024]{2,1,0:T(8,128)(2,1)S(1)} %copy-done.5, bf16[64,8,2048]{2,1,0:T(8,128)(2,1)S(1)} %all_to_all.5), kind=kOutput, calls=%fused_computation.10 | convolution fusion | flops 2147483648 | bytes 8388608 | tf_op jit(solution)/shard_map/dot_general | solution.py:39
  53.1 0.0 all-reduce.5.cloned.1.call-update
  53.1 0.0 copy-start.4
  53.1 0.0 all-reduce.7.cloned.1.call-start
  53.2 3.1 fusion
  56.3 2.5 psum.67
  58.8 17.8 %all-reduce.5.cloned.1.call-done = f32[512,1024]{1,0:T(8,128)} async-done(((f32[512,1024]{1,0:T(8,128)}), f32[512,1024]{1,0:T(8,128)}) %all-reduce.5.cloned.1.call-update) | async-done | bytes 2097168 | tf_op jit(solution)/shard_map/psum | solution.py:42
  76.5 3.6 %multiply_reduce_fusion.1 = (f32[]{:T(128)}, f32[1024]{0:T(1024)S(1)}, bf16[512,1024]{1,0:T(8,128)(2,1)S(1)}) fusion(f32[1024]{0:T(1024)S(1)} %psum.67, s32[512,1024]{1,0:T(8,128)} %param.11, f32[512,1024]{1,0:T(8,128)} %all-reduce.5.cloned.1.call-done, f32[1024]{0:T(1024)S(1)} %copy-done.4), kind=kLoop, calls=%fused_computation.19 | loop fusion | flops 3668991 | bytes 5255172 | tf_op jit(solution)/shard_map/reduce_sum | solution.py:66
  80.1 4.4 %fusion.6 = f32[512,2048]{1,0:T(8,128)} fusion(bf16[1,1024,2048]{2,1,0:T(8,128)(2,1)S(1)} %copy-done, bf16[512,1024]{1,0:T(8,128)(2,1)S(1)} %get-tuple-element.8), kind=kOutput, calls=%fused_computation.8 | convolution fusion | flops 2147483648 | bytes 9437184 | tf_op jit(solution)/shard_map/dot_general | solution.py:49
  84.5 0.0 all-reduce.7.cloned.1.call-update
  84.5 0.0 all-reduce.9.cloned.1.call-start
  84.6 105.1 %all-reduce.7.cloned.1.call-done = f32[512,2048]{1,0:T(8,128)} async-done(((f32[512,2048]{1,0:T(8,128)}), f32[512,2048]{1,0:T(8,128)}) %all-reduce.7.cloned.1.call-update) | async-done | bytes 4194320 | tf_op jit(solution)/shard_map/psum | solution.py:50
  189.7 0.0 all-reduce.9.cloned.1.call-update
  189.7 0.0 all-reduce.11.cloned.1.call-start
  189.7 94.9 %all-reduce.9.cloned.1.call-done = f32[512,2048]{1,0:T(8,128)} async-done(((f32[512,2048]{1,0:T(8,128)}), f32[512,2048]{1,0:T(8,128)}) %all-reduce.9.cloned.1.call-update) | async-done | bytes 4194320 | tf_op jit(solution)/shard_map/psum | solution.py:50
  284.6 0.0 copy-done.3
  284.6 4.0 %multiply_reduce_fusion = (f32[]{:T(128)}, bf16[512,2048]{1,0:T(8,128)(2,1)S(1)}) fusion(f32[512,2048]{1,0:T(8,128)} %all-reduce.9.cloned.1.call-done, bf16[64,8,2048]{2,1,0:T(8,128)(2,1)S(1)} %all_to_all.5, f32[2048]{0:T(1024)S(1)} %bitcast.32), kind=kLoop, calls=%fused_computation.12 | loop fusion | flops 6291455 | bytes 8396804 | tf_op jit(solution)/shard_map/reduce_sum | solution.py:53
  288.7 1.3 copy-done.2
  290.0 3.7 %fusion.4 = f32[512,1024]{1,0:T(8,128)} fusion(bf16[512,2048]{1,0:T(8,128)(2,1)S(1)} %get-tuple-element.10, bf16[1,1024,2048]{2,1,0:T(8,128)(2,1)S(1)} %copy-done.1), kind=kOutput, calls=%fused_computation.6 | convolution fusion | flops 2147483648 | bytes 8388608 | tf_op jit(solution)/shard_map/td,fd->tf/dot_general | solution.py:54
  293.7 0.0 all-reduce.11.cloned.1.call-update
  295.0 3.0 psum.68
  298.0 9.2 %psum.69 = f32[]{:T(128)} all-reduce(f32[]{:T(128)} %psum.68), channel_id=1, replica_groups=mesh['layer'=2,'latent_0'=4,'latent_1'=4,'latent_2'=4] {'latent_0'}, use_global_device_ids=true, to_apply=%region_10.11 | all-reduce | flops 1 | bytes 8 | tf_op jit(solution)/shard_map/psum | solution.py:30
  307.2 11.0 %psum.70 = f32[]{:T(128)} all-reduce(f32[]{:T(128)} %psum.69), channel_id=1, replica_groups=mesh['layer'=2,'latent_0'=4,'latent_1'=4,'latent_2'=4] {'latent_1'}, use_global_device_ids=true, to_apply=%region_11.12 | all-reduce | flops 1 | bytes 8 | tf_op jit(solution)/shard_map/psum | solution.py:30
  318.2 11.5 %psum.71 = f32[]{:T(128)} all-reduce(f32[]{:T(128)} %psum.70), channel_id=1, replica_groups=mesh['layer'=2,'latent_0'=4,'latent_1'=4,'latent_2'=4] {'latent_2'}, use_global_device_ids=true, to_apply=%region_12.13 | all-reduce | flops 1 | bytes 8 | tf_op jit(solution)/shard_map/psum | solution.py:30
  330.3 6.6 %fusion.10 = bf16[1,1024,2048]{2,1,0:T(8,128)(2,1)} fusion(f32[1024]{0:T(1024)S(1)} %add_sqrt_fusion, bf16[1,1024,2048]{2,1,0:T(8,128)(2,1)} %param.9, f32[1024]{0:T(1024)S(1)} %broadcast_multiply_fusion, bf16[512,2048]{1,0:T(8,128)(2,1)} %copy-done.2, bf16[512,1024]{1,0:T(8,128)(2,1)S(1)} %get-tuple-element.8), kind=kOutput, calls=%fused_computation.15 | convolution fusion | flops 2157969408 | bytes 11542528 | tf_op jit(solution)/shard_map/tf,td->fd/dot_general | solution.py:63
  337.0 6.7 %convert_bitcast_fusion = bf16[1,2048,1024]{1,2,0:T(8,128)(2,1)} fusion(bf16[64,8,2048]{2,1,0:T(8,128)(2,1)S(1)} %all_to_all.5, f32[512,1024]{1,0:T(8,128)} %all-reduce.11.cloned.1.call-done, s32[512,1024]{1,0:T(8,128)} %param.11, f32[1024]{0:T(1024)S(1)} %broadcast_multiply_fusion.1), kind=kOutput, calls=%fused_computation.13 | convolution fusion | flops 2151677952 | bytes 10489856 | tf_op jit(solution)/shard_map/td,tf->df/dot_general | solution.py:57
  343.7 6.4 %copy.9 = bf16[1,2048,1024]{2,1,0:T(8,128)(2,1)} copy(bf16[1,2048,1024]{1,2,0:T(8,128)(2,1)} %convert_bitcast_fusion) | data formatting | bytes 8388608
  (11 shorter events, 0.0 us)
Async XLA Ops:
  7.2 69.4 %all-reduce.5.cloned.1.call-start = ((), (), s32[]{:S(2)}) async-start(), calls=%async_computation.1 | async-start | bytes 4194304 | tf_op jit(solution)/shard_map/psum | solution.py:42
  8.2 41.2 %copy-start.5 = (bf16[1,2048,1024]{2,1,0:T(8,128)(2,1)S(1)}, bf16[1,2048,1024]{2,1,0:T(8,128)(2,1)}, u32[]{:S(2)}) copy-start(bf16[1,2048,1024]{2,1,0:T(8,128)(2,1)} %param.7) | copy-start | bytes 12582916
  53.1 23.4 %copy-start.4 = (f32[1024]{0:T(1024)S(1)}, f32[1024]{0:T(1024)}, u32[]{:S(2)}) copy-start(f32[1024]{0:T(1024)} %param.8) | copy-start | bytes 12292
  53.1 136.5 %all-reduce.7.cloned.1.call-start = ((), (), s32[]{:S(2)}) async-start(), calls=%async_computation.2 | async-start | bytes 8388608 | tf_op jit(solution)/shard_map/psum | solution.py:50
  76.5 3.6 %copy-start = (bf16[1,1024,2048]{2,1,0:T(8,128)(2,1)S(1)}, bf16[1,1024,2048]{2,1,0:T(8,128)(2,1)}, u32[]{:S(2)}) copy-start(bf16[1,1024,2048]{2,1,0:T(8,128)(2,1)} %param.9) | copy-start | bytes 12582916
  84.5 200.1 %all-reduce.9.cloned.1.call-start = ((), (), s32[]{:S(2)}) async-start(), calls=%async_computation.3 | async-start | bytes 8388608 | tf_op jit(solution)/shard_map/psum | solution.py:50
  189.6 95.0 %copy-start.3 = (f32[1,2048]{1,0:T(1,128)S(1)}, f32[1,2048]{1,0:T(1,128)}, u32[]{:S(2)}) copy-start(f32[1,2048]{1,0:T(1,128)} %param.10) | copy-start | bytes 24580
  189.7 147.3 %all-reduce.11.cloned.1.call-start = ((), (), s32[]{:S(2)}) async-start(), calls=%async_computation.4 | async-start | bytes 4194304 | tf_op jit(solution)/shard_map/psum | solution.py:55
  284.6 5.4 %copy-start.1 = (bf16[1,1024,2048]{2,1,0:T(8,128)(2,1)S(1)}, bf16[1,1024,2048]{2,1,0:T(8,128)(2,1)}, u32[]{:S(2)}) copy-start(bf16[1,1024,2048]{2,1,0:T(8,128)(2,1)} %param.9) | copy-start | bytes 12582916
  288.7 1.4 copy-start.2
Sparse Core Ops, SparseCore 0:
  53.3 23.2 all-reduce.4
  84.7 104.9 all-reduce.6
  192.1 92.4 all-reduce.8
  293.9 26.5 all-reduce.10
